TPU v7x, 256 devices: a whole 4x4x8 slice. The times are simulated.
256 devices in a mesh: dp: 32 (over z, x), tensor: 8 (over y, core).
Axes of the slice: x: 4, y: 4, z: 8, core: 2. Of those that a mesh axis runs over, the one named last changes fastest.
Arguments:
- tokens: bfloat16 [65536, 8192], P('dp', 'tensor'), may hold values from -6 to 6
- base_value_weight: bfloat16 [8192, 1024], P('tensor'), may hold values from -0.0625 to 0.0625
- adapter_down_weight: bfloat16 [512, 8192, 64], P('dp', 'tensor'), may hold values from -0.0625 to 0.0625
- adapter_up_weight: bfloat16 [512, 64, 1024], P('dp', None, 'tensor'), may hold values from -0.75 to 0.75
- request_adapter_index: int32 [128], P('dp'), may hold values from 0 to 511
- storage_index_table: int32 [512], replicated, may hold values from 0 to 511, each once
Outputs:
- values_out: bfloat16 [65536, 1024], P('dp', 'tensor')
Inputs may be any that keep to these rules, and one draw needn't show every extreme that they name: `request_adapter_index`: each adapter id names an adapter. storage_index_table is a permutation of the storage positions.
All inputs are finite; a program needn't handle non-finite values.
Results may differ from a plain program's by a relative error of at most 0.003.
Values may be sent and summed in bfloat16 or wider, within the bound.
A program may use at most 128 MiB of HBM per device.

v0:
```python
import jax
import jax.numpy as jnp
from jax import lax
from jax.sharding import PartitionSpec as P

adapter_scale = 0.5


def shards(
    tokens,
    base_value_weight,
    adapter_down_weight,
    adapter_up_weight,
    request_adapter_index,
    storage_index_table,
):
    n_rows, width = tokens.shape
    requests_here = request_adapter_index.shape[0]
    seq_len = n_rows // requests_here
    owned = adapter_down_weight.shape[0]
    rank = adapter_down_weight.shape[2]
    local_columns = adapter_up_weight.shape[2]
    n_dp = lax.axis_size("dp")
    down_t = jnp.swapaxes(adapter_down_weight, 1, 2)
    pieces = jnp.concatenate(
        (
            down_t.reshape(owned, n_dp, rank * width // n_dp // 128, 128),
            adapter_up_weight.reshape(owned, n_dp, rank * local_columns // n_dp // 128, 128),
        ),
        axis=2,
    )
    pieces = jnp.swapaxes(pieces, 0, 1)
    held = lax.all_to_all(pieces, "dp", split_axis=0, concat_axis=0, tiled=True)
    held = held.reshape(n_dp * owned, -1, 128)
    every_id = lax.all_gather(request_adapter_index, "dp", axis=0, tiled=True)
    positions = storage_index_table[every_id]
    outgoing = held[positions].reshape(n_dp, requests_here, -1, 128)
    fetched = lax.all_to_all(outgoing, "dp", split_axis=0, concat_axis=0, tiled=True)
    fetched = jnp.swapaxes(fetched, 0, 1)
    down_rows = rank * width // n_dp // 128
    down_sel = fetched[:, :, :down_rows].reshape(requests_here, rank, width)
    up_sel = fetched[:, :, down_rows:].reshape(requests_here, rank, local_columns)
    base_projection = lax.psum_scatter(
        lax.dot_general(
            base_value_weight, tokens, (((0,), (1,)), ((), ())), preferred_element_type=jnp.float32
        ),
        "tensor",
        scatter_dimension=0,
        tiled=True,
    ).T
    grouped = tokens.reshape(requests_here, seq_len, width)
    low_part = jnp.einsum("rsd,rkd->rks", grouped, down_sel, preferred_element_type=jnp.float32)
    low = lax.psum(low_part, "tensor").astype(jnp.bfloat16)
    adapter_update = jnp.einsum("rks,rkc->rsc", low, up_sel, preferred_element_type=jnp.float32)
    adapter_update = adapter_update.reshape(n_rows, local_columns)
    return (base_projection + adapter_scale * adapter_update).astype(jnp.bfloat16)


def solution(mesh):
    return jax.shard_map(
        shards,
        mesh=mesh,
        in_specs=(
            P("dp", "tensor"),
            P("tensor", None),
            P("dp", "tensor", None),
            P("dp", None, "tensor"),
            P("dp"),
            P(),
        ),
        out_specs=P("dp", "tensor"),
        check_vma=False,
    )
```

profile of v0, /device:TPU:2, one launch (start us, length us, event | category | flops | bytes accessed | tf_op | source)
XLA Modules:
  0.0 181.0 jit_solution(14180586535549913768)
XLA Ops:
  6.5 1.6 copy-done
  8.1 9.0 %fusion.3 = f32[1024,2048]{1,0:T(8,128)} fusion(bf16[1024,1024]{1,0:T(8,128)(2,1)S(1)} %copy-done, bf16[2048,1024]{1,0:T(8,128)(2,1)} %param.6), kind=kOutput, calls=%fused_computation.12 | convolution fusion | flops 4294967296 | bytes 14680064 | tf_op jit(solution)/shard_map/dot_general | solution.py:44
  17.1 4.2 %reshape.37 = bf16[16,32,16,128]{3,2,1,0:T(8,128)(2,1)} reshape(bf16[16,64,1024]{2,1,0:T(8,128)(2,1)} %bitcast.33) | data formatting | bytes 4194304 | tf_op jit(solution)/shard_map/reshape | solution.py:27
  21.4 2.4 %maximum_bitcast_fusion = bf16[32,16,18,128]{3,2,0,1:T(8,128)(2,1)S(1)} fusion(bf16[16,32,2,128]{3,2,1,0:T(2,128)(2,1)S(1)} %bitcast.35, bf16[16,32,16,128]{3,2,1,0:T(8,128)(2,1)} %reshape.37), kind=kLoop, calls=%fused_computation.2 | loop fusion | flops 4718592 | bytes 4718592 | tf_op jit(solution)/shard_map/transpose | solution.py:32
  23.8 4.2 %copy.23 = bf16[32,16,18,128]{3,1,2,0:T(8,128)(2,1)} copy(bf16[32,16,18,128]{3,2,0,1:T(8,128)(2,1)S(1)} %maximum_bitcast_fusion) | data formatting | bytes 4718592 | tf_op jit(solution)/shard_map/transpose | solution.py:32
  28.0 11.8 %all-to-all-start = ((bf16[32,16,18,128]{3,1,2,0:T(8,128)(2,1)}), bf16[32,16,18,128]{3,1,2,0:T(8,128)(2,1)}, u32[]{:S(2)}, u32[]{:S(2)}) async-start(bf16[32,16,18,128]{3,1,2,0:T(8,128)(2,1)} %copy.23), calls=%async_computation.1 | async-start | bytes 4718592 | tf_op jit(solution)/shard_map/all_to_all | solution.py:33
  39.8 0.6 dynamic-slice
  41.0 0.2 dynamic-update-slice
  41.3 57.8 %all-reduce = s32[128]{0:T(128)S(1)} all-reduce(s32[128]{0:T(128)S(1)} %dynamic-update-slice), channel_id=1, replica_groups=mesh['dp'=32,'tensor'=8] {'dp'}, use_global_device_ids=true, to_apply=%add | all-reduce | flops 128 | bytes 1024
  99.1 1.3 gather_fusion
  100.4 2.3 %copy.24 = bf16[32,16,18,128]{3,1,0,2:T(8,128)(2,1)S(1)} copy(bf16[32,16,18,128]{3,1,2,0:T(8,128)(2,1)} %all-to-all-done) | data formatting | bytes 4718592 | tf_op jit(solution)/shard_map/all_to_all | solution.py:33
  102.7 3.4 %copy.25 = bf16[512,18,128]{2,1,0:T(8,128)(2,1)} copy(bf16[512,18,128]{2,0,1:T(8,128)(2,1)S(1)} %bitcast.27) | data formatting | bytes 4718592 | tf_op jit(solution)/shard_map/reshape | solution.py:34
  106.1 2.6 %gather_fusion.1 = bf16[128,18,128]{2,1,0:T(8,128)(2,1)S(1)} fusion(bf16[512,18,128]{2,1,0:T(8,128)(2,1)} %copy.25, s32[1024]{0:T(1024)S(1)} %pad_clamp_fusion), kind=kCustom, calls=%fused_computation.1 | custom fusion | bytes 1180160 | tf_op jit(solution)/shard_map/gather | solution.py:37
  108.7 0.2 copy.27
  108.9 24.5 %all_to_all.10 = bf16[32,4,18,128]{3,1,2,0:T(4,128)(2,1)S(1)} all-to-all(bf16[32,4,18,128]{3,1,2,0:T(4,128)(2,1)S(1)} %copy.27), channel_id=1, replica_groups=mesh['dp'=32,'tensor'=8] {'dp'}, dimensions={0} | all-to-all | bytes 1179648 | tf_op jit(solution)/shard_map/all_to_all | solution.py:38
  133.5 0.3 slice.12
  133.8 0.1 copy.28
  133.8 0.2 reshape.41
  134.1 3.6 %fusion.4 = f32[4,64,512]{2,1,0:T(8,128)S(1)} fusion(bf16[4,64,1024]{2,1,0:T(8,128)(2,1)S(1)} %reshape.41, bf16[4,512,1024]{2,1,0:T(8,128)(2,1)} %bitcast.28), kind=kOutput, calls=%fused_computation.13 | convolution fusion | flops 268435456 | bytes 5242880 | tf_op jit(solution)/shard_map/rsd,rkd->rks/dot_general | solution.py:52
  137.7 29.3 %all-reduce.2 = bf16[4,64,512]{2,1,0:T(8,128)(2,1)S(1)} all-reduce(f32[4,64,512]{2,1,0:T(8,128)S(1)} %fusion.4), channel_id=1, replica_groups=mesh['dp'=32,'tensor'=8] {'tensor'}, use_global_device_ids=true, to_apply=%region_1.0 | all-reduce | flops 131072 | bytes 786432 | tf_op jit(solution)/shard_map/psum | solution.py:53
  167.0 1.4 convolution_multiply_fusion
  168.4 1.6 copy.35
  170.0 2.1 %fusion = bf16[2048,128]{0,1:T(8,128)(2,1)} fusion(f32[2048,128]{0,1:T(8,128)S(1)} %copy.35, f32[128,2048]{1,0:T(8,128)} %reduce-scatter.2.cloned.1.call-done), kind=kLoop, calls=%fused_computation.5 | loop fusion | flops 524288 | bytes 2621440 | tf_op jit(solution)/shard_map/convert_element_type | solution.py:56
  172.1 2.0 %copy.31 = bf16[2048,128]{1,0:T(8,128)(2,1)} copy(bf16[2048,128]{0,1:T(8,128)(2,1)} %fusion) | data formatting | bytes 1048576 | tf_op jit(solution)/shard_map/convert_element_type | solution.py:56
  (20 shorter events, 0.2 us)
Async XLA Ops:
  6.5 1.6 copy-start
  6.5 163.4 %reduce-scatter.2.cloned.1.call-start = ((), (), s32[]{:S(2)}) async-start(), calls=%async_computation.3 | async-start | bytes 9437184 | tf_op jit(solution)/shard_map/reduce_scatter | solution.py:43
  17.1 4.3 %copy-start.2 = (bf16[16,64,128]{2,1,0:T(8,128)(2,1)S(1)}, bf16[16,64,128]{2,1,0:T(8,128)(2,1)}, u32[]{:S(2)}) copy-start(bf16[16,64,128]{2,1,0:T(8,128)(2,1)} %param.9) | copy-start | bytes 786436
  27.9 11.8 %copy-start.4 = (u32[256]{0:T(256)S(1)}, u32[256]{0:T(256)}, u32[]{:S(2)}) copy-start(u32[256]{0:T(256)} %constant.11) | copy-start | bytes 3076
  28.0 13.1 %copy-start.3 = (s32[4]{0:T(128)S(1)}, s32[4]{0:T(128)}, u32[]{:S(2)}) copy-start(s32[4]{0:T(128)} %param.10) | copy-start | bytes 52
  28.0 71.1 %copy-start.1 = (s32[512]{0:T(512)S(1)}, s32[512]{0:T(512)}, u32[]{:S(2)}) copy-start(s32[512]{0:T(512)} %param.11) | copy-start | bytes 6148
  28.0 72.4 %all-to-all-start = ((bf16[32,16,18,128]{3,1,2,0:T(8,128)(2,1)}), bf16[32,16,18,128]{3,1,2,0:T(8,128)(2,1)}, u32[]{:S(2)}, u32[]{:S(2)}) async-start(bf16[32,16,18,128]{3,1,2,0:T(8,128)(2,1)} %copy.23), calls=%async_computation.1 | async-start | bytes 4718592 | tf_op jit(solution)/shard_map/all_to_all | solution.py:33
Sparse Core Ops, SparseCore 0:
  17.2 57.9 reduce-scatter.1
where the time goes:
time: 182 us; the launch traced here: 181 us
  blocking collectives  112 us (62%)
  local copies, waits for them, and re-layouts  24.9 us (14%)
  between operations  14.2 us (8%)
  matrix products  13.9 us (8%)
  starting transfers between devices  11.8 us (6%)
  other arithmetic  4.53 us (2%)
    unnamed x1, blocking collectives  57.8 us
    psum x1, blocking collectives, shards(): low = lax.psum(low_part, 'tensor').astype(jnp.bfloat16)  29.3 us
    all_to_all x1, blocking collectives, shards(): lax.all_to_all(outgoing, 'dp', split_axis=0, concat_axis=0, tiled=True)  24.5 us
    all_to_all x1, starting transfers between devices, shards(): held = lax.all_to_all(pieces, 'dp', split_axis=0, concat_axis=0, tiled=True)  11.8 us
    dot_general x1, matrix products, shards(): lax.dot_general(base_value_weight, tokens, (((0,), (1,)), ((), ())), pref...  8.96 us
    reshape x1, local copies, waits for them, and re-layouts, shards(): down_t.reshape(owned, n_dp, rank * width // n_dp // 128, 128)  4.24 us
    transpose x1, local copies, waits for them, and re-layouts, shards(): pieces = jnp.swapaxes(pieces, 0, 1)  4.18 us
  transfers between devices with their start and end apart: 2, of which 0 were waited for; matrix products, arithmetic and copies ran while one was open for 16% of the time, Pallas kernels for 0%

commit v1 on v0

--- a/solution.py
+++ b/solution.py
@@ -2,6 +2,7 @@
 import jax.numpy as jnp
 from jax import lax
 from jax.sharding import PartitionSpec as P
+from jax.lax import all_gather
 
 adapter_scale = 0.5
 
@@ -50,7 +51,7 @@
     ).T
     grouped = tokens.reshape(requests_here, seq_len, width)
     low_part = jnp.einsum("rsd,rkd->rks", grouped, down_sel, preferred_element_type=jnp.float32)
-    low = lax.psum(low_part, "tensor").astype(jnp.bfloat16)
+    low = jnp.sum(all_gather(low_part, "tensor"), 0).astype(jnp.bfloat16)
     adapter_update = jnp.einsum("rks,rkc->rsc", low, up_sel, preferred_element_type=jnp.float32)
     adapter_update = adapter_update.reshape(n_rows, local_columns)
     return (base_projection + adapter_scale * adapter_update).astype(jnp.bfloat16)

time: 182 us -> 231 us (1.27)
  waiting for transfers between devices: 0.04 us -> 74.3 us
  blocking collectives: 112 us -> 82.2 us
  other arithmetic: 4.53 us -> 7.24 us
    reduce_scatter x1, waiting for transfers between devices: 0.02 us -> 51.9 us  [shards(): lax.psum_scatter(lax.dot_general(base_value_weight, tokens, (((0,), (1,))...]
    psum x1 -> x0, blocking collectives: 29.3 us -> none  [shards(): low = lax.psum(low_part, 'tensor').astype(jnp.bfloat16)]
    all_gather x0 -> x1, waiting for transfers between devices: none -> 22.4 us  [shards(): low = jnp.sum(all_gather(low_part, 'tensor'), 0).astype(jnp.bfloat16)]
    reduce_sum x0 -> x1, other arithmetic: none -> 2.69 us  [shards(): low = jnp.sum(all_gather(low_part, 'tensor'), 0).astype(jnp.bfloat16)]
  transfers between devices with their start and end apart: 2 -> 3, of which waited for: 0 -> 2; matrix products, arithmetic and copies ran while one was open for 16% -> 7% of each run, Pallas kernels for 0% -> 0%
where the time goes in v1:
time: 231 us; the launch traced here: 230 us
  blocking collectives  82.2 us (36%)
  waiting for transfers between devices  74.3 us (32%)
  local copies, waits for them, and re-layouts  25 us (11%)
  matrix products  14.8 us (6%)
  between operations  14.2 us (6%)
  starting transfers between devices  12.1 us (5%)
  other arithmetic  7.24 us (3%)
    unnamed x1, blocking collectives  57.7 us
    reduce_scatter x1, waiting for transfers between devices, shards(): lax.psum_scatter(lax.dot_general(base_value_weight, tokens, (((0,), (1,))...  51.9 us
    all_to_all x1, blocking collectives, shards(): lax.all_to_all(outgoing, 'dp', split_axis=0, concat_axis=0, tiled=True)  24.5 us
    all_gather x1, waiting for transfers between devices, shards(): low = jnp.sum(all_gather(low_part, 'tensor'), 0).astype(jnp.bfloat16)  22.4 us
    all_to_all x1, starting transfers between devices, shards(): held = lax.all_to_all(pieces, 'dp', split_axis=0, concat_axis=0, tiled=True)  11.8 us
    dot_general x1, matrix products, shards(): lax.dot_general(base_value_weight, tokens, (((0,), (1,)), ((), ())), pref...  8.99 us
  transfers between devices with their start and end apart: 3, of which 2 were waited for; matrix products, arithmetic and copies ran while one was open for 7% of the time, Pallas kernels for 0%

profile of v1, /device:TPU:2, one launch (start us, length us, event | category | flops | bytes accessed | tf_op | source)
XLA Modules:
  0.0 229.9 jit_solution(12391628966867068021)
XLA Ops:
  6.5 4.3 %reshape.37 = bf16[16,32,16,128]{3,2,1,0:T(8,128)(2,1)} reshape(bf16[16,64,1024]{2,1,0:T(8,128)(2,1)} %bitcast.35) | data formatting | bytes 4194304 | tf_op jit(solution)/shard_map/reshape | solution.py:28
  10.8 2.4 %maximum_bitcast_fusion = bf16[32,16,18,128]{3,2,0,1:T(8,128)(2,1)S(1)} fusion(bf16[16,32,2,128]{3,2,1,0:T(2,128)(2,1)S(1)} %bitcast.37, bf16[16,32,16,128]{3,2,1,0:T(8,128)(2,1)} %reshape.37), kind=kLoop, calls=%fused_computation.2 | loop fusion | flops 4718592 | bytes 4718592 | tf_op jit(solution)/shard_map/transpose | solution.py:33
  13.2 4.1 %copy.24 = bf16[32,16,18,128]{3,1,2,0:T(8,128)(2,1)} copy(bf16[32,16,18,128]{3,2,0,1:T(8,128)(2,1)S(1)} %maximum_bitcast_fusion) | data formatting | bytes 4718592 | tf_op jit(solution)/shard_map/transpose | solution.py:33
  17.4 11.8 %all-to-all-start = ((bf16[32,16,18,128]{3,1,2,0:T(8,128)(2,1)}), bf16[32,16,18,128]{3,1,2,0:T(8,128)(2,1)}, u32[]{:S(2)}, u32[]{:S(2)}) async-start(bf16[32,16,18,128]{3,1,2,0:T(8,128)(2,1)} %copy.24), calls=%async_computation.1 | async-start | bytes 4718592 | tf_op jit(solution)/shard_map/all_to_all | solution.py:34
  29.3 0.6 dynamic-slice
  30.5 0.2 dynamic-update-slice
  30.8 57.7 %all-reduce = s32[128]{0:T(128)S(1)} all-reduce(s32[128]{0:T(128)S(1)} %dynamic-update-slice), channel_id=1, replica_groups=mesh['dp'=32,'tensor'=8] {'dp'}, use_global_device_ids=true, to_apply=%add | all-reduce | flops 128 | bytes 1024
  88.5 1.3 gather_fusion
  89.8 2.3 copy.25
  92.1 3.3 %copy.26 = bf16[512,18,128]{2,1,0:T(8,128)(2,1)} copy(bf16[512,18,128]{2,0,1:T(8,128)(2,1)S(1)} %bitcast.28) | data formatting | bytes 4718592 | tf_op jit(solution)/shard_map/reshape | solution.py:35
  95.4 2.6 %gather_fusion.1 = bf16[128,18,128]{2,1,0:T(8,128)(2,1)S(1)} fusion(bf16[512,18,128]{2,1,0:T(8,128)(2,1)} %copy.26, s32[1024]{0:T(1024)S(1)} %pad_clamp_fusion), kind=kCustom, calls=%fused_computation.1 | custom fusion | bytes 1180160 | tf_op jit(solution)/shard_map/gather | solution.py:38
  98.3 24.5 %all_to_all.10 = bf16[32,4,18,128]{3,1,2,0:T(4,128)(2,1)S(1)} all-to-all(bf16[32,4,18,128]{3,1,2,0:T(4,128)(2,1)S(1)} %copy.28), channel_id=1, replica_groups=mesh['dp'=32,'tensor'=8] {'dp'}, dimensions={0} | all-to-all | bytes 1179648 | tf_op jit(solution)/shard_map/all_to_all | solution.py:39
  122.8 0.3 slice.12
  123.0 0.9 copy.29
  123.9 1.3 reshape.41
  125.2 4.4 %fusion.4 = f32[4,64,512]{2,1,0:T(8,128)} fusion(bf16[4,64,1024]{2,1,0:T(8,128)(2,1)S(1)} %reshape.41, bf16[4,512,1024]{2,1,0:T(8,128)(2,1)} %bitcast.29), kind=kOutput, calls=%fused_computation.13 | convolution fusion | flops 268435456 | bytes 5242880 | tf_op jit(solution)/shard_map/rsd,rkd->rks/dot_general | solution.py:53
  129.8 9.0 %fusion.3 = f32[1024,2048]{1,0:T(8,128)} fusion(bf16[1024,1024]{1,0:T(8,128)(2,1)S(1)} %copy-done, bf16[2048,1024]{1,0:T(8,128)(2,1)} %param.6), kind=kOutput, calls=%fused_computation.12 | convolution fusion | flops 4294967296 | bytes 14680064 | tf_op jit(solution)/shard_map/dot_general | solution.py:45
  138.9 22.4 %all-gather.3.cloned.1.call-done = f32[32,64,512]{2,1,0:T(8,128)} async-done(((f32[4,64,512]{2,1,0:T(8,128)}), f32[32,64,512]{2,1,0:T(8,128)}) %all-gather.3.cloned.1.call-update) | async-done | bytes 4194320 | tf_op jit(solution)/shard_map/all_gather | solution.py:54
  161.3 2.7 %reduce_sum.9 = bf16[4,64,512]{2,1,0:T(8,128)(2,1)S(1)} reduce(f32[8,4,64,512]{3,2,1,0:T(8,128)} %bitcast.30, f32[]{:T(128)} %constant.2.clone.1), dimensions={0}, to_apply=%region_1.0 | reduce | flops 917504 | bytes 4456452 | tf_op jit(solution)/shard_map/reduce_sum | solution.py:54
  164.0 1.4 convolution_multiply_fusion
  165.4 1.6 copy.36
  167.0 51.9 %reduce-scatter.2.cloned.1.call-done = f32[128,2048]{1,0:T(8,128)} async-done(((f32[1024,2048]{1,0:T(8,128)}), f32[128,2048]{1,0:T(8,128)}) %reduce-scatter.2.cloned.1.call-update) | async-done | bytes 1048592 | tf_op jit(solution)/shard_map/reduce_scatter | solution.py:44
  218.9 2.1 fusion
  221.0 2.0 copy.32
  (23 shorter events, 0.7 us)
Async XLA Ops:
  6.5 123.3 %copy-start = (bf16[1024,1024]{1,0:T(8,128)(2,1)S(1)}, bf16[1024,1024]{1,0:T(8,128)(2,1)}, u32[]{:S(2)}) copy-start(bf16[1024,1024]{1,0:T(8,128)(2,1)} %param.7) | copy-start | bytes 6291460
  6.5 4.3 %copy-start.2 = (bf16[16,64,128]{2,1,0:T(8,128)(2,1)S(1)}, bf16[16,64,128]{2,1,0:T(8,128)(2,1)}, u32[]{:S(2)}) copy-start(bf16[16,64,128]{2,1,0:T(8,128)(2,1)} %param.9) | copy-start | bytes 786436
  17.4 11.9 %copy-start.4 = (u32[256]{0:T(256)S(1)}, u32[256]{0:T(256)}, u32[]{:S(2)}) copy-start(u32[256]{0:T(256)} %constant.13) | copy-start | bytes 3076
  17.4 13.1 %copy-start.3 = (s32[4]{0:T(128)S(1)}, s32[4]{0:T(128)}, u32[]{:S(2)}) copy-start(s32[4]{0:T(128)} %param.10) | copy-start | bytes 52
  17.4 71.1 %copy-start.1 = (s32[512]{0:T(512)S(1)}, s32[512]{0:T(512)}, u32[]{:S(2)}) copy-start(s32[512]{0:T(512)} %param.11) | copy-start | bytes 6148
  17.4 72.4 %all-to-all-start = ((bf16[32,16,18,128]{3,1,2,0:T(8,128)(2,1)}), bf16[32,16,18,128]{3,1,2,0:T(8,128)(2,1)}, u32[]{:S(2)}, u32[]{:S(2)}) async-start(bf16[32,16,18,128]{3,1,2,0:T(8,128)(2,1)} %copy.24), calls=%async_computation.1 | async-start | bytes 4718592 | tf_op jit(solution)/shard_map/all_to_all | solution.py:34
  29.2 132.1 %all-gather.3.cloned.1.call-start = ((), (), s32[]{:S(2)}) async-start(), calls=%async_computation.4 | async-start | bytes 4718592 | tf_op jit(solution)/shard_map/all_gather | solution.py:54
  129.6 89.3 %reduce-scatter.2.cloned.1.call-start = ((), (), s32[]{:S(2)}) async-start(), calls=%async_computation.3 | async-start | bytes 9437184 | tf_op jit(solution)/shard_map/reduce_scatter | solution.py:44
Sparse Core Ops, SparseCore 0:
  129.7 31.5 all-gather.2
  163.9 54.9 reduce-scatter.1
